TPU v7x, 32 devices: a whole 2x2x4 slice. The times are simulated.
32 devices in a mesh: grp: 16 (over z, x, core), shard: 2 (over y).
Axes of the slice: x: 2, y: 2, z: 4, core: 2. Of those that a mesh axis runs over, the one named last changes fastest.
Arguments:
- tokens: bfloat16 [2, 32, 1024, 768], P(None, ('grp', 'shard')), may hold values from -6 to 6
- segments: int32 [2, 32, 1024], P(None, ('grp', 'shard')), may hold values from 0 to 15, never falling along the last dimension, each value on 1 to 512 neighbouring positions
- embed_grad: float32 [2, 32, 1024, 128], P(None, ('grp', 'shard')), may hold values from -67.88225 to 67.88225
- qkv_weight: bfloat16 [768, 2304], P(('grp', 'shard')), may hold values from -0.21875 to 0.21875
- query_bias: bfloat16 [768], P(('grp', 'shard')), may hold values from -3 to 3
- value_bias: bfloat16 [768], P(('grp', 'shard')), may hold values from -3 to 3
- out_weight: bfloat16 [768, 768], P(('grp', 'shard')), may hold values from -0.625 to 0.625
- out_bias: bfloat16 [768], P(('grp', 'shard')), may hold values from -1.75 to 1.75
- norm1_gain: bfloat16 [768], P(('grp', 'shard')), may hold values from 0.25 to 1.75
- norm1_bias: bfloat16 [768], P(('grp', 'shard')), may hold values from -1.75 to 1.75
- up_weight: bfloat16 [768, 3072], P(('grp', 'shard')), may hold values from -0.21875 to 0.21875
- up_bias: bfloat16 [3072], P(('grp', 'shard')), may hold values from -3 to 3
- down_weight: bfloat16 [3072, 768], P(('grp', 'shard')), may hold values from -0.15625 to 0.15625
- down_bias: bfloat16 [768], P(('grp', 'shard')), may hold values from -1.75 to 1.75
- norm2_gain: bfloat16 [768], P(('grp', 'shard')), may hold values from 0.25 to 1.75
- norm2_bias: bfloat16 [768], P(('grp', 'shard')), may hold values from -1.75 to 1.75
- proj_weight: bfloat16 [768, 128], P(('grp', 'shard')), may hold values from -0.21875 to 0.21875
Outputs:
- embed: float32 [2, 32, 1024, 128], P(None, ('grp', 'shard'))
- input_grad: float32 [2, 32, 1024, 768], P(None, ('grp', 'shard'))
- qkv_weight_grad: float32 [768, 2304], P(('grp', 'shard'))
- query_bias_grad: float32 [768], P(('grp', 'shard'))
- value_bias_grad: float32 [768], P(('grp', 'shard'))
- out_weight_grad: float32 [768, 768], P(('grp', 'shard'))
- out_bias_grad: float32 [768], P(('grp', 'shard'))
- norm1_gain_grad: float32 [768], P(('grp', 'shard'))
- norm1_bias_grad: float32 [768], P(('grp', 'shard'))
- up_weight_grad: float32 [768, 3072], P(('grp', 'shard'))
- up_bias_grad: float32 [3072], P(('grp', 'shard'))
- down_weight_grad: float32 [3072, 768], P(('grp', 'shard'))
- down_bias_grad: float32 [768], P(('grp', 'shard'))
- norm2_gain_grad: float32 [768], P(('grp', 'shard'))
- norm2_bias_grad: float32 [768], P(('grp', 'shard'))
- proj_weight_grad: float32 [768, 128], P(('grp', 'shard'))
Inputs may be any that keep to these rules, and one draw needn't show every extreme that they name: `segments`: segment numbers never fall along a sequence; every number of 0 to 15 appears, each on 1 to 512 positions, one on exactly 512.
All inputs are finite; a program needn't handle non-finite values.
Results may differ from a plain program's by a relative error of at most 0.017.
Values may be sent and summed in bfloat16 or wider, within the bound.
No kernel may reach another device: no remote copies, remote signals or barrier semaphores. Data moves between devices by JAX's collectives and lax.ppermute only.
A program may use at most 256 MiB of HBM per device.

v0:
```python
import jax
import jax.numpy as jnp
from jax import lax
from jax.sharding import PartitionSpec as P

HEADS = 12
HEAD = 64


NEG_FILL = -1e30
NORM_EPS = 1e-12
EMBED_EPS = 1e-06
SQRT_HALF = 0.7071067811865476
INV_ROOT_TAU = 0.3989422804014327


def product(left, right):
    return jnp.dot(left, right, preferred_element_type=jnp.float32)


def product_tn(left, right):
    return lax.dot_general(
        left, right, (((0,), (0,)), ((), ())), preferred_element_type=jnp.float32
    )


def product_nt(left, right):
    return lax.dot_general(
        left, right, (((1,), (1,)), ((), ())), preferred_element_type=jnp.float32
    )


def norm_forward(hidden, gain, shift):
    center = hidden - jnp.mean(hidden, axis=-1, keepdims=True)
    inverse = lax.rsqrt(jnp.mean(center * center, axis=-1, keepdims=True) + NORM_EPS)
    normed = center * inverse
    return (normed * gain + shift, normed, inverse)


def norm_backward(grad_out, normed, inverse, gain):
    scaled = grad_out * gain
    return inverse * (
        scaled
        - jnp.mean(scaled, axis=-1, keepdims=True)
        - normed * jnp.mean(scaled * normed, axis=-1, keepdims=True)
    )


def split_heads(matrix):
    return matrix.reshape(matrix.shape[0], HEADS, HEAD).transpose(1, 0, 2)


def merge_heads(stacked):
    return stacked.transpose(1, 0, 2).reshape(stacked.shape[1], HEADS * HEAD)


def masked_scores(query_head, key_head, same_doc):
    scores = product_nt(query_head, key_head) * float(HEAD) ** (-0.5)
    return jnp.where(same_doc, scores, NEG_FILL)


def sequence_pass(full, tokens_in, segment_ids, cotangent):
    (
        qkv_weight,
        query_bias,
        value_bias,
        out_weight,
        out_bias,
        norm1_gain,
        norm1_bias,
        up_weight,
        up_bias,
        down_weight,
        down_bias,
        norm2_gain,
        norm2_bias,
        proj_weight,
    ) = full
    width = qkv_weight.shape[0]
    scale = float(HEAD) ** (-0.5)
    same_doc = segment_ids[:, None] == segment_ids[None, :]
    gain_one = norm1_gain.astype(jnp.float32)
    gain_two = norm2_gain.astype(jnp.float32)
    bias_row = jnp.concatenate([query_bias, jnp.zeros_like(query_bias), value_bias]).astype(
        jnp.float32
    )
    joined = (product(tokens_in, qkv_weight) + bias_row).astype(jnp.bfloat16)
    query_heads = split_heads(joined[:, :width])
    key_heads = split_heads(joined[:, width : 2 * width])
    value_heads = split_heads(joined[:, 2 * width :])

    def head_forward(parts):
        query_head, key_head, value_head = parts
        scores = masked_scores(query_head, key_head, same_doc)
        row_max = jnp.max(scores, axis=1, keepdims=True)
        expo = jnp.exp(scores - row_max)
        denom_sum = jnp.sum(expo, axis=1, keepdims=True)
        attn_probs = (expo / denom_sum).astype(jnp.bfloat16)
        return (product(attn_probs, value_head), row_max + jnp.log(denom_sum))

    head_out, log_sums = lax.map(head_forward, (query_heads, key_heads, value_heads))
    context = merge_heads(head_out).astype(jnp.bfloat16)
    attn_branch = product(context, out_weight) + out_bias.astype(jnp.float32)
    first_out, first_normed, first_inverse = norm_forward(
        tokens_in.astype(jnp.float32) + attn_branch, gain_one, norm1_bias.astype(jnp.float32)
    )
    first_low = first_out.astype(jnp.bfloat16)
    pre_act = product(first_low, up_weight) + up_bias.astype(jnp.float32)
    normal_cdf = 0.5 * (1.0 + lax.erf(pre_act * SQRT_HALF))
    act_low = (pre_act * normal_cdf).astype(jnp.bfloat16)
    ffn_branch = product(act_low, down_weight) + down_bias.astype(jnp.float32)
    second_out, second_normed, second_inverse = norm_forward(
        first_low.astype(jnp.float32) + ffn_branch, gain_two, norm2_bias.astype(jnp.float32)
    )
    second_low = second_out.astype(jnp.bfloat16)
    projected = product(second_low, proj_weight)
    inv_length = lax.rsqrt(jnp.sum(projected * projected, axis=-1, keepdims=True) + EMBED_EPS)
    embedded = projected * inv_length
    grad_proj = (
        inv_length * cotangent
        - projected * inv_length**3 * jnp.sum(cotangent * projected, axis=-1, keepdims=True)
    ).astype(jnp.bfloat16)
    proj_grad = product_tn(second_low, grad_proj)
    grad_second = product_nt(grad_proj, proj_weight)
    gain_two_grad = jnp.sum(grad_second * second_normed, axis=0)
    shift_two_grad = jnp.sum(grad_second, axis=0)
    grad_res_two = norm_backward(grad_second, second_normed, second_inverse, gain_two)
    grad_ffn = grad_res_two.astype(jnp.bfloat16)
    down_bias_grad = jnp.sum(grad_ffn.astype(jnp.float32), axis=0)
    down_grad = product_tn(act_low, grad_ffn)
    act_slope = normal_cdf + pre_act * jnp.exp(-0.5 * pre_act * pre_act) * INV_ROOT_TAU
    grad_pre = (product_nt(grad_ffn, down_weight) * act_slope).astype(jnp.bfloat16)
    up_bias_grad = jnp.sum(grad_pre.astype(jnp.float32), axis=0)
    up_grad = product_tn(first_low, grad_pre)
    grad_first = grad_res_two + product_nt(grad_pre, up_weight)
    gain_one_grad = jnp.sum(grad_first * first_normed, axis=0)
    shift_one_grad = jnp.sum(grad_first, axis=0)
    grad_res_one = norm_backward(grad_first, first_normed, first_inverse, gain_one)
    grad_attn = grad_res_one.astype(jnp.bfloat16)
    out_bias_grad = jnp.sum(grad_attn.astype(jnp.float32), axis=0)
    out_grad = product_tn(context, grad_attn)
    grad_context = split_heads(product_nt(grad_attn, out_weight).astype(jnp.bfloat16))

    def head_backward(parts):
        query_head, key_head, value_head, grad_head, log_sum = parts
        scores = masked_scores(query_head, key_head, same_doc)
        attn_full = jnp.exp(scores - log_sum)
        grad_probs = product_nt(grad_head, value_head)
        grad_scores = (
            attn_full * (grad_probs - jnp.sum(attn_full * grad_probs, axis=1, keepdims=True))
        ).astype(jnp.bfloat16)
        grad_query = product(grad_scores, key_head) * scale
        grad_key = product_tn(grad_scores, query_head) * scale
        grad_value = product_tn(attn_full.astype(jnp.bfloat16), grad_head)
        return (grad_query, grad_key, grad_value)

    grad_queries, grad_keys, grad_values = lax.map(
        head_backward, (query_heads, key_heads, value_heads, grad_context, log_sums)
    )
    grad_joined = jnp.concatenate(
        [merge_heads(grad_queries), merge_heads(grad_keys), merge_heads(grad_values)], axis=1
    ).astype(jnp.bfloat16)
    column_sums = jnp.sum(grad_joined.astype(jnp.float32), axis=0)
    qkv_grad = product_tn(tokens_in, grad_joined)
    input_grad = grad_res_one + product_nt(grad_joined, qkv_weight)
    grads = (
        qkv_grad,
        column_sums[:width],
        column_sums[2 * width :],
        out_grad,
        out_bias_grad,
        gain_one_grad,
        shift_one_grad,
        up_grad,
        up_bias_grad,
        down_grad,
        down_bias_grad,
        gain_two_grad,
        shift_two_grad,
        proj_grad,
    )
    return (embedded, input_grad, grads)


def local(
    tokens,
    segments,
    embed_grad,
    qkv_weight,
    query_bias,
    value_bias,
    out_weight,
    out_bias,
    norm1_gain,
    norm1_bias,
    up_weight,
    up_bias,
    down_weight,
    down_bias,
    norm2_gain,
    norm2_bias,
    proj_weight,
):
    group_count = lax.axis_size("grp")
    shard_count = lax.axis_size("shard")
    local_pieces = (
        qkv_weight,
        query_bias,
        value_bias,
        out_weight,
        out_bias,
        norm1_gain,
        norm1_bias,
        up_weight,
        up_bias,
        down_weight,
        down_bias,
        norm2_gain,
        norm2_bias,
        proj_weight,
    )
    totals = tuple(
        (
            jnp.zeros((piece.shape[0] * group_count * shard_count,) + piece.shape[1:], jnp.float32)
            for piece in local_pieces
        )
    )
    embed_parts = []
    grad_parts = []
    for micro in range(tokens.shape[0]):
        full = (
            lax.all_gather(qkv_weight, ("grp", "shard"), axis=0, tiled=True),
            lax.all_gather(query_bias, ("grp", "shard"), axis=0, tiled=True),
            lax.all_gather(value_bias, ("grp", "shard"), axis=0, tiled=True),
            lax.all_gather(out_weight, ("grp", "shard"), axis=0, tiled=True),
            lax.all_gather(out_bias, ("grp", "shard"), axis=0, tiled=True),
            lax.all_gather(norm1_gain, ("grp", "shard"), axis=0, tiled=True),
            lax.all_gather(norm1_bias, ("grp", "shard"), axis=0, tiled=True),
            lax.all_gather(up_weight, ("grp", "shard"), axis=0, tiled=True),
            lax.all_gather(up_bias, ("grp", "shard"), axis=0, tiled=True),
            lax.all_gather(down_weight, ("grp", "shard"), axis=0, tiled=True),
            lax.all_gather(down_bias, ("grp", "shard"), axis=0, tiled=True),
            lax.all_gather(norm2_gain, ("grp", "shard"), axis=0, tiled=True),
            lax.all_gather(norm2_bias, ("grp", "shard"), axis=0, tiled=True),
            lax.all_gather(proj_weight, ("grp", "shard"), axis=0, tiled=True),
        )

        def seq_step(running, seq_item):
            embedded, input_grad, grads = sequence_pass(full, seq_item[0], seq_item[1], seq_item[2])
            return (
                tuple((total + part for total, part in zip(running, grads))),
                (embedded, input_grad),
            )

        totals, (embedded_all, token_grads) = lax.scan(
            seq_step, totals, (tokens[micro], segments[micro], embed_grad[micro])
        )
        embed_parts.append(embedded_all)
        grad_parts.append(token_grads)
    reduced = lax.psum_scatter(totals, ("grp", "shard"), scatter_dimension=0, tiled=True)
    return (jnp.stack(embed_parts), jnp.stack(grad_parts)) + tuple(reduced)


def solution(mesh):
    placed = (
        P(None, ("grp", "shard"), None, None),
        P(None, ("grp", "shard"), None),
        P(None, ("grp", "shard"), None, None),
        P(("grp", "shard"), None),
        P(("grp", "shard")),
        P(("grp", "shard")),
        P(("grp", "shard"), None),
        P(("grp", "shard")),
        P(("grp", "shard")),
        P(("grp", "shard")),
        P(("grp", "shard"), None),
        P(("grp", "shard")),
        P(("grp", "shard"), None),
        P(("grp", "shard")),
        P(("grp", "shard")),
        P(("grp", "shard")),
        P(("grp", "shard"), None),
    )
    return jax.shard_map(
        local,
        mesh=mesh,
        in_specs=placed,
        out_specs=(
            P(None, ("grp", "shard"), None, None),
            P(None, ("grp", "shard"), None, None),
            P(("grp", "shard"), None),
            P(("grp", "shard")),
            P(("grp", "shard")),
            P(("grp", "shard"), None),
            P(("grp", "shard")),
            P(("grp", "shard")),
            P(("grp", "shard")),
            P(("grp", "shard"), None),
            P(("grp", "shard")),
            P(("grp", "shard"), None),
            P(("grp", "shard")),
            P(("grp", "shard")),
            P(("grp", "shard")),
            P(("grp", "shard"), None),
        ),
        check_vma=False,
    )
```

profile of v0, /device:TPU:0, one launch (start us, length us, event | category | flops | bytes accessed | tf_op | source)
XLA Modules:
  0.0 1251.6 jit_solution(7569999918055715558)
XLA Ops:
  18.3 42.6 %all-reduce.20 = (bf16[768]{0:T(1024)(128)(2,1)S(1)}, bf16[768]{0:T(1024)(128)(2,1)S(1)}, bf16[768]{0:T(1024)(128)(2,1)S(1)}, bf16[768]{0:T(1024)(128)(2,1)S(1)}...) all-reduce(bf16[768]{0:T(1024)(128)(2,1)S(1)} %dynamic-update-slice, ...), channel_id=1, replica_groups=mesh['grp'=16,'shard'=2] {'grp','shard'}, use_global_device_ids=true, to_apply=%add.1 | all-reduce | flops 9216 | bytes 36864
  68.0 72.0 %all_gather.69 = bf16[768,128]{1,0:T(8,128)(2,1)} all-gather(bf16[24,128]{1,0:T(8,128)(2,1)S(1)} %copy-done.47), channel_id=1, replica_groups=mesh['grp'=16,'shard'=2] {'grp','shard'}, dimensions={0}, use_global_device_ids=true | all-gather | bytes 202752 | tf_op jit(solution)/shard_map/all_gather | solution.py:245
  174.3 68.3 %while.75 = (s32[]{:T(128)}, bf16[12,1024,64]{1,2,0:T(8,128)(2,1)}, f32[12,1024,1]{1,2,0:T(1,128)S(1)}, bf16[12,1024,64]{2,1,0:T(8,128)(2,1)S(1)}, bf16[12,1024,...) while((s32[]{:T(128)}, bf16[12,1024,64]{1,2,0:T(8,128)(2,1)}, ...), condition=%wide.region_12.13_spmd.clone, body=%wide.region_9.12_spmd.clone.sunk | while | flops 284163072 | bytes 13695065 | solution.py:101
  242.6 7.5 add_convert_fusion.1
  273.0 68.7 %while.74 = (s32[]{:T(128)}, bf16[12,1024,64]{1,2,0:T(8,128)(2,1)}, f32[12,1024,1]{1,2,0:T(1,128)S(1)}, bf16[12,1024,64]{2,1,0:T(8,128)(2,1)}, bf16[12,1024,64]{...) while((s32[]{:T(128)}, bf16[12,1024,64]{1,2,0:T(8,128)(2,1)}, ...), condition=%wide.region_3.4_spmd.clone, body=%wide.region_0.3_spmd.clone.sunk | while | flops 284163072 | bytes 13695065 | solution.py:101
  355.6 8.2 fusion.152
  368.4 12.8 %multiply_convert_fusion.3 = (bf16[1024,3072]{1,0:T(8,128)(2,1)}, bf16[1024,3072]{1,0:T(8,128)(2,1)}, f32[1024,3072]{1,0:T(8,128)}) fusion(f32[3072]{0:T(1024)S(1)} %convert_element_type.225, f32[1024,3072]{1,0:T(8,128)S(1)} %fusion.152, bf16[1024,768]{0,1:T(8,128)(2,1)S(1)} %get-tuple-element.750, bf16[768,3072]{1,0:T(8,128)(2,1)S(1)} %copy-done.5), kind=kOutput, calls=%fused_computation.132 | convolution fusion | flops 4869586944 | bytes 44052480 | tf_op jit(solution)/shard_map/while/body/eval_jaxpr/dot_general | solution.py:18
  381.3 9.0 fusion.148
  425.9 16.6 %convert_reduce_fusion.1 = (f32[3072]{0:T(1024)}, bf16[1024,3072]{1,0:T(8,128)(2,1)}) fusion(f32[1024,3072]{1,0:T(8,128)} %get-tuple-element.769, f32[3072]{0:T(1024)S(1)} %convert_element_type.225, bf16[3072,768]{1,0:T(8,128)(2,1)} %all-gather.11.cloned.1.call-done, f32[1024,768]{0,1:T(8,128)S(1)} %get-tuple-element.717), kind=kOutput, calls=%fused_computation.129 | convolution fusion | flops 4873516032 | bytes 26763264 | tf_op jit(solution)/shard_map/while/body/eval_jaxpr/dot_general | solution.py:28
  442.5 10.1 multiply_reduce_fusion.5
  454.3 14.2 %convert_reduce_fusion = (f32[3072]{0:T(1024)}, bf16[1024,3072]{1,0:T(8,128)(2,1)}) fusion(f32[1024,3072]{1,0:T(8,128)S(1)} %bitcast.320, f32[3072]{0:T(1024)S(1)} %convert_element_type.225, bf16[3072,768]{1,0:T(8,128)(2,1)} %all-gather.11.cloned.1.call-done, f32[1024,768]{0,1:T(8,128)S(1)} %get-tuple-element.715), kind=kOutput, calls=%fused_computation.128 | convolution fusion | flops 4873516032 | bytes 26763264 | tf_op jit(solution)/shard_map/while/body/eval_jaxpr/dot_general | solution.py:28
  468.6 11.9 convert_reduce_fusion.7
  496.7 149.1 %while.76 = (s32[]{:T(128)}, bf16[12,1024,64]{1,2,0:T(8,128)(2,1)}, bf16[12,1024,64]{1,2,0:T(8,128)(2,1)}, bf16[12,1024,64]{1,2,0:T(8,128)(2,1)}, bf16[12,1024,6...) while((s32[]{:T(128)}, bf16[12,1024,64]{1,2,0:T(8,128)(2,1)}, ...), condition=%wide.region_25.26_spmd.clone, body=%wide.region_23.25_spmd.clone.sunk | while | flops 681704448 | bytes 34112624 | solution.py:157
  665.1 156.9 %while.77 = (s32[]{:T(128)}, bf16[12,1024,64]{1,2,0:T(8,128)(2,1)}, bf16[12,1024,64]{1,2,0:T(8,128)(2,1)}, bf16[12,1024,64]{1,2,0:T(8,128)(2,1)}, bf16[12,1024,6...) while((s32[]{:T(128)}, bf16[12,1024,64]{1,2,0:T(8,128)(2,1)}, ...), condition=%wide.region_33.34_spmd.clone, body=%wide.region_31.33_spmd.clone.sunk | while | flops 681704448 | bytes 34112624 | solution.py:157
  828.8 8.2 add_bitcast_fusion
  836.9 8.0 copy.138
  845.0 8.9 fusion.134
  854.0 11.0 convolution_add_fusion
  865.1 7.9 fusion.153
  873.0 10.5 convolution_add_fusion.1
  889.2 39.4 %all-reduce.19 = (f32[768]{0:T(1024)S(1)}, f32[768]{0:T(1024)S(1)}, f32[768]{0:T(1024)S(1)}, f32[768]{0:T(1024)S(1)}, f32[768]{0:T(1024)S(1)}, /*index=5*/f32[30...) all-reduce(f32[768]{0:T(1024)S(1)} %get-tuple-element.745, ...), channel_id=3, replica_groups=mesh['grp'=16,'shard'=2] {'grp','shard'}, use_global_device_ids=true, to_apply=%region_37.38.clone | all-reduce | flops 9216 | bytes 73728
  933.4 8.4 add_bitcast_fusion.2
  961.0 142.4 %reduce-scatter.14.cloned.1.call-done = f32[96,768]{1,0:T(8,128)} async-done(((f32[3072,768]{1,0:T(8,128)}), f32[96,768]{1,0:T(8,128)}) %reduce-scatter.14.cloned.1.call-update) | async-done | bytes 294928 | tf_op jit(solution)/shard_map/reduce_scatter | solution.py:260
  1103.4 141.2 %reduce-scatter.12.cloned.1.call-done = f32[24,3072]{1,0:T(8,128)} async-done(((f32[768,3072]{1,0:T(8,128)}), f32[24,3072]{1,0:T(8,128)}) %reduce-scatter.12.cloned.1.call-update) | async-done | bytes 294928 | tf_op jit(solution)/shard_map/reduce_scatter | solution.py:260
  (575 shorter events, 643.7 us)
Async XLA Ops:
  7.2 139.2 %all-gather.5.cloned.1.call-start = ((), (), s32[]{:S(2)}) async-start(), calls=%async_computation.5 | async-start | bytes 3649536 | tf_op jit(solution)/shard_map/all_gather | solution.py:232
  7.9 333.8 %all-gather.7.cloned.1.call-start = ((), (), s32[]{:S(2)}) async-start(), calls=%async_computation.6 | async-start | bytes 1216512 | tf_op jit(solution)/shard_map/all_gather | solution.py:235
  8.7 346.9 %all-gather.9.cloned.1.call-start = ((), (), s32[]{:S(2)}) async-start(), calls=%async_computation.7 | async-start | bytes 4866048 | tf_op jit(solution)/shard_map/all_gather | solution.py:239
  9.4 371.8 %all-gather.11.cloned.1.call-start = ((), (), s32[]{:S(2)}) async-start(), calls=%async_computation.8 | async-start | bytes 4866048 | tf_op jit(solution)/shard_map/all_gather | solution.py:241
  10.0 949.1 %reduce-scatter.18.cloned.1.call-start = ((), (), s32[]{:S(2)}) async-start(), calls=%async_computation.13 | async-start | bytes 405504
  66.2 80.2 %copy-start.26 = (bf16[2,1,1024,768]{3,2,1,0:T(8,128)(2,1)S(1)}, bf16[2,1,1024,768]{3,2,1,0:T(8,128)(2,1)}, u32[]{:S(2)}) copy-start(bf16[2,1,1024,768]{3,2,1,0:T(8,128)(2,1)} %param.25) | copy-start | bytes 9437188
  355.5 25.7 %copy-start.12 = (bf16[1024,768]{0,1:T(8,128)(2,1)}, bf16[1024,768]{0,1:T(8,128)(2,1)S(1)}, u32[]{:S(2)}) copy-start(bf16[1024,768]{0,1:T(8,128)(2,1)S(1)} %get-tuple-element.750) | copy-start | bytes 4718596
  355.6 12.8 %copy-start.5 = (bf16[768,3072]{1,0:T(8,128)(2,1)S(1)}, bf16[768,3072]{1,0:T(8,128)(2,1)}, u32[]{:S(2)}) copy-start(bf16[768,3072]{1,0:T(8,128)(2,1)} %all-gather.9.cloned.1.call-done) | copy-start | bytes 14155780
  368.4 12.9 %copy-start.53 = (f32[768]{0:T(1024)S(1)}, f32[768]{0:T(1024)}, u32[]{:S(2)}) copy-start(f32[768]{0:T(1024)} %convert_element_type.227) | copy-start | bytes 9220
  381.2 9.1 copy-start.13
  408.3 550.7 %reduce-scatter.10.cloned.1.call-start = ((), (), s32[]{:S(2)}) async-start(), calls=%async_computation.9 | async-start | bytes 2433024 | tf_op jit(solution)/shard_map/reduce_scatter | solution.py:260
  420.2 22.3 %slice-start.3 = ((s8[4718592]{0:T(1024)(128)(4,1)}), s8[4194304]{0:T(1024)(128)(4,1)S(1)}, s32[]{:S(2)}) async-start(s8[4718592]{0:T(1024)(128)(4,1)} %bitcast.321), calls=%async_computation.17 | async-start | bytes 8388608
  425.8 16.6 %copy-start.30 = (f32[1024,768]{0,1:T(8,128)}, f32[1024,768]{0,1:T(8,128)S(1)}, u32[]{:S(2)}) copy-start(f32[1024,768]{0,1:T(8,128)S(1)} %get-tuple-element.717) | copy-start | bytes 9437188
  425.8 16.6 %slice-start.4 = ((s8[4718592]{0:T(1024)(128)(4,1)}), s8[524288]{0:T(1024)(128)(4,1)S(1)}, s32[]{:S(2)}) async-start(s8[4718592]{0:T(1024)(128)(4,1)} %bitcast.321), calls=%async_computation.18 | async-start | bytes 1048576
  425.8 16.6 %copy-start.7 = (f32[1024,768]{0,1:T(8,128)S(1)}, f32[1024,768]{0,1:T(8,128)}, u32[]{:S(2)}) copy-start(f32[1024,768]{0,1:T(8,128)} %copy-done.6) | copy-start | bytes 9437188
  425.8 28.5 %slice-start = ((s8[12582912]{0:T(1024)(128)(4,1)}), s8[4194304]{0:T(1024)(128)(4,1)S(1)}, s32[]{:S(2)}) async-start(s8[12582912]{0:T(1024)(128)(4,1)} %bitcast.319), calls=%async_computation.14 | async-start | bytes 8388608
  425.9 28.5 %slice-start.1 = ((s8[12582912]{0:T(1024)(128)(4,1)}), s8[4194304]{0:T(1024)(128)(4,1)S(1)}, s32[]{:S(2)}) async-start(s8[12582912]{0:T(1024)(128)(4,1)} %bitcast.319), calls=%async_computation.15 | async-start | bytes 8388608
  442.5 10.1 copy-start.4
  442.5 11.8 slice-start.2
  454.3 14.3 %copy-start.28 = (f32[1024,768]{0,1:T(8,128)}, f32[1024,768]{0,1:T(8,128)S(1)}, u32[]{:S(2)}) copy-start(f32[1024,768]{0,1:T(8,128)S(1)} %get-tuple-element.715) | copy-start | bytes 9437188
  454.3 14.3 %copy-start.3 = (f32[1024,768]{0,1:T(8,128)S(1)}, f32[1024,768]{0,1:T(8,128)}, u32[]{:S(2)}) copy-start(f32[1024,768]{0,1:T(8,128)} %copy-done.2) | copy-start | bytes 9437188
  660.8 300.2 %reduce-scatter.16.cloned.1.call-start = ((), (), s32[]{:S(2)}) async-start(), calls=%async_computation.12 | async-start | bytes 7299072
  845.0 258.4 %reduce-scatter.14.cloned.1.call-start = ((), (), s32[]{:S(2)}) async-start(), calls=%async_computation.11 | async-start | bytes 9732096 | tf_op jit(solution)/shard_map/reduce_scatter | solution.py:260
  865.0 379.6 %reduce-scatter.12.cloned.1.call-start = ((), (), s32[]{:S(2)}) async-start(), calls=%async_computation.10 | async-start | bytes 9732096 | tf_op jit(solution)/shard_map/reduce_scatter | solution.py:260
  (50 other events, 208.7 us)
Sparse Core Ops, SparseCore 0:
  10.9 63.1 all-gather.4
  77.0 52.9 all-gather.6
  133.0 62.6 all-gather.8
  198.4 62.4 all-gather.10
  408.5 90.6 reduce-scatter.17
  661.0 94.8 reduce-scatter.9
  845.1 115.8 reduce-scatter.15
  968.5 134.8 reduce-scatter.13
  1109.9 134.6 reduce-scatter.11
where the time goes:
time: 1260 us; the launch traced here: 1250 us
  matrix products  582 us (46%)
  waiting for transfers between devices  288 us (23%)
  blocking collectives  154 us (12%)
  local copies, waits for them, and re-layouts  128 us (10%)
  other arithmetic  82.5 us (7%)
  between operations  15.3 us (1%)
    reduce_scatter x3, waiting for transfers between devices, local(): lax.psum_scatter(totals, ('grp', 'shard'), scatter_dimension=0, tiled=True)  284 us
    dot_general x82, matrix products, product_nt(): lax.dot_general(left, right, (((1,), (1,)), ((), ())), preferred_element_...  222 us
    dot_general x58, matrix products, product(): return jnp.dot(left, right, preferred_element_type=jnp.float32)  180 us
    dot_general x58, matrix products, product_tn(): lax.dot_general(left, right, (((0,), (0,)), ((), ())), preferred_element_...  180 us
    unnamed x2, blocking collectives  82 us
    all_gather x1, blocking collectives, local(): lax.all_gather(proj_weight, ('grp', 'shard'), axis=0, tiled=True)  72 us
    unnamed x171, local copies, waits for them, and re-layouts  68.1 us
    convert_element_type x24, other arithmetic, head_backward(): grad_scores = (attn_full * (grad_probs - jnp.sum(attn_full * grad_probs,...  27.2 us
  transfers between devices with their start and end apart: 9, of which 3 were waited for; matrix products, arithmetic and copies ran while one was open for 60% of the time, Pallas kernels for 0%

commit v1 on v0

v1 whole, which is shorter than its diff:
```python
import functools

import jax
import jax.numpy as jnp
from jax import lax
from jax.experimental import pallas as pl
from jax.experimental.pallas import tpu as pltpu
from jax.sharding import PartitionSpec as P

F32, BF16 = jnp.float32, jnp.bfloat16
HEADS = 12
HEAD = 64
NEG = -1e30
NORM_EPS = 1e-12
EMBED_EPS = 1e-06
SQRT_HALF = 0.7071067811865476
INV_ROOT_TAU = 0.3989422804014327


def nn(left, right):
    return lax.dot_general(left, right, (((1,), (0,)), ((), ())), preferred_element_type=F32)


def nt(left, right):
    return lax.dot_general(left, right, (((1,), (1,)), ((), ())), preferred_element_type=F32)


def tn(left, right):
    return lax.dot_general(left, right, (((0,), (0,)), ((), ())), preferred_element_type=F32)


def norm_forward(hidden, gain, shift):
    center = hidden - jnp.mean(hidden, axis=-1, keepdims=True)
    inverse = lax.rsqrt(jnp.mean(center * center, axis=-1, keepdims=True) + NORM_EPS)
    normed = center * inverse
    return (normed * gain + shift, normed, inverse)


def norm_backward(grad_out, normed, inverse, gain):
    scaled = grad_out * gain
    return inverse * (
        scaled
        - jnp.mean(scaled, axis=-1, keepdims=True)
        - normed * jnp.mean(scaled * normed, axis=-1, keepdims=True)
    )


def fwd_kernel(lo_ref, hi_ref, segc_ref, segr_ref, q_ref, k_ref, v_ref, ctx_ref, lse_ref, vt, *, qt, kb, pairs):
    s = pl.program_id(0)
    n = q_ref.shape[0]
    low = lax.broadcasted_iota(jnp.int32, (1, 128), 1) < 64
    for p in range(pairs):
        vt[pl.ds(p * 128, 128), :] = v_ref[:, p * 128:(p + 1) * 128].T

    def tile(i, _):
        qs = pl.ds(pl.multiple_of(i * qt, qt), qt)
        segq = segr_ref[0, :, qs]
        lo = lo_ref[s, i]
        cnt = hi_ref[s, i] - lo

        def body(c):
            nk = c * kb
            ks = pl.ds(pl.multiple_of(lo * kb, kb), nk)
            same = segc_ref[0, ks, :] == segq
            for p in range(pairs):
                cols = slice(p * 128, (p + 1) * 128)
                q = q_ref[qs, cols] * jnp.asarray(0.125, BF16)
                zero = jnp.zeros_like(q)
                outs = []
                for hh in range(2):
                    h = 2 * p + hh
                    qm = jnp.where(low, q, zero) if hh == 0 else jnp.where(low, zero, q)
                    sc = jnp.where(same, nt(k_ref[ks, cols], qm), NEG)
                    m = jnp.max(sc, axis=0, keepdims=True)
                    e = jnp.exp(sc - m)
                    l = jnp.sum(e, axis=0, keepdims=True)
                    pv = nn(vt[h * 64:(h + 1) * 64, ks], e.astype(BF16))
                    outs.append(pv / l)
                    lse_ref[0, h:h + 1, qs] = m + jnp.log(l)
                ctx_ref[qs, cols] = jnp.concatenate(outs, axis=0).T.astype(BF16)

        for c in range(1, n // kb + 1):
            pl.when(cnt == c)(functools.partial(body, c))
        return 0

    lax.fori_loop(0, n // qt, tile, 0)


def attn_fwd(joined, segments, lo, hi, *, qt, kb, pairs):
    nseq, n = segments.shape
    width = joined.shape[1] // 3
    nb = width // (128 * pairs)
    segc = segments[:, :, None]
    segr = segments[:, None, :]
    w = 128 * pairs
    return pl.pallas_call(
        functools.partial(fwd_kernel, qt=qt, kb=kb, pairs=pairs),
        grid_spec=pltpu.PrefetchScalarGridSpec(
            num_scalar_prefetch=2, grid=(nseq, nb),
            in_specs=[
                pl.BlockSpec((1, n, 1), lambda s, p, *_: (s, 0, 0)),
                pl.BlockSpec((1, 1, n), lambda s, p, *_: (s, 0, 0)),
                pl.BlockSpec((n, w), lambda s, p, *_: (s, p)),
                pl.BlockSpec((n, w), lambda s, p, *_: (s, nb + p)),
                pl.BlockSpec((n, w), lambda s, p, *_: (s, 2 * nb + p)),
            ],
            out_specs=[
                pl.BlockSpec((n, w), lambda s, p, *_: (s, p)),
                pl.BlockSpec((1, 2 * pairs, n), lambda s, p, *_: (s * nb + p, 0, 0)),
            ],
            scratch_shapes=[pltpu.VMEM((w, n), BF16)],
        ),
        out_shape=[jax.ShapeDtypeStruct((nseq * n, width), BF16),
                   jax.ShapeDtypeStruct((nseq * nb, 2 * pairs, n), F32)],
        compiler_params=pltpu.CompilerParams(vmem_limit_bytes=48 << 20),
        name="attn_fwd",
    )(lo, hi, segc, segr, joined, joined, joined)


def bwd_kernel(lo_ref, hi_ref, segc_ref, segr_ref, q_ref, k_ref, v_ref, ctx_ref, do_ref, lse_ref, out_ref,
               kt, qt_t, dot_t, dk, dv, *, qt, kb, pairs, form):
    s = pl.program_id(0)
    n = q_ref.shape[0]
    low = lax.broadcasted_iota(jnp.int32, (1, 128), 1) < 64
    for p in range(pairs):
        cols = slice(p * 128, (p + 1) * 128)
        kt[pl.ds(p * 128, 128), :] = k_ref[:, cols].T
        if form == "B":
            qt_t[pl.ds(p * 128, 128), :] = (q_ref[:, cols] * jnp.asarray(0.125, BF16)).T
            dot_t[pl.ds(p * 128, 128), :] = do_ref[:, cols].T
    dk[...] = jnp.zeros_like(dk)
    dv[...] = jnp.zeros_like(dv)
    sel = jnp.where((lax.broadcasted_iota(jnp.int32, (8, 128), 1) // 64) == lax.broadcasted_iota(jnp.int32, (8, 128), 0), 1.0, 0.0).astype(F32)

    def tile(i, _):
        qs = pl.ds(pl.multiple_of(i * qt, qt), qt)
        segq = segr_ref[0, :, qs]
        lo = lo_ref[s, i]
        cnt = hi_ref[s, i] - lo

        def body(c):
            nk = c * kb
            ks = pl.ds(pl.multiple_of(lo * kb, kb), nk)
            same = segc_ref[0, ks, :] == segq
            for p in range(pairs):
                cols = slice(p * 128, (p + 1) * 128)
                q = q_ref[qs, cols] * jnp.asarray(0.125, BF16)
                do = do_ref[qs, cols]
                zero = jnp.zeros_like(q)
                prod = do.astype(F32) * ctx_ref[qs, cols].astype(F32)
                d8 = lax.dot_general(sel, prod, (((1,), (1,)), ((), ())), preferred_element_type=F32, precision=lax.Precision.HIGHEST)
                kblk, vblk = k_ref[ks, cols], v_ref[ks, cols]
                dqs = []
                dvs = dks = None
                for hh in range(2):
                    h = 2 * p + hh
                    mask = (lambda t: jnp.where(low, t, zero)) if hh == 0 else (lambda t: jnp.where(low, zero, t))
                    qm, dom = mask(q), mask(do)
                    sc = nt(kblk, qm) - lse_ref[0, h:h + 1, qs]
                    pt = jnp.exp(jnp.where(same, sc, NEG))
                    dp = nt(vblk, dom)
                    ds = (pt * (dp - d8[hh:hh + 1])).astype(BF16)
                    ptl = pt.astype(BF16)
                    hr = slice(h * 64, (h + 1) * 64)
                    if form == "A":
                        a, b = nn(ptl, dom), nn(ds, qm)
                        dvs = a if dvs is None else dvs + a
                        dks = b if dks is None else dks + b
                    else:
                        dv[hr, ks] += nt(dot_t[hr, qs], ptl)
                        dk[hr, ks] += nt(qt_t[hr, qs], ds)
                    dqs.append(nn(kt[hr, ks], ds))
                if form == "A":
                    dv[ks, cols] += dvs
                    dk[ks, cols] += dks
                out_ref[0, qs, cols] = (jnp.concatenate(dqs, axis=0).T * 0.125).astype(BF16)

        for c in range(1, n // kb + 1):
            pl.when(cnt == c)(functools.partial(body, c))
        return 0

    lax.fori_loop(0, n // qt, tile, 0)
    if form == "A":
        out_ref[1] = dk[...].astype(BF16)
        out_ref[2] = dv[...].astype(BF16)
    else:
        for p in range(pairs):
            cols = slice(p * 128, (p + 1) * 128)
            out_ref[1, :, cols] = dk[cols, :].T.astype(BF16)
            out_ref[2, :, cols] = dv[cols, :].T.astype(BF16)


def attn_bwd(joined, ctx, dctx, lse, segments, lo, hi, *, qt, kb, pairs, form="A"):
    nseq, n = segments.shape
    width = joined.shape[1] // 3
    nb = width // (128 * pairs)
    segc = segments[:, :, None]
    segr = segments[:, None, :]
    w = 128 * pairs
    acc = (n, w) if form == "A" else (w, n)
    tr = (w, n) if form == "B" else (8, 128)
    return pl.pallas_call(
        functools.partial(bwd_kernel, qt=qt, kb=kb, pairs=pairs, form=form),
        grid_spec=pltpu.PrefetchScalarGridSpec(
            num_scalar_prefetch=2, grid=(nseq, nb),
            in_specs=[
                pl.BlockSpec((1, n, 1), lambda s, p, *_: (s, 0, 0)),
                pl.BlockSpec((1, 1, n), lambda s, p, *_: (s, 0, 0)),
                pl.BlockSpec((n, w), lambda s, p, *_: (s, p)),
                pl.BlockSpec((n, w), lambda s, p, *_: (s, nb + p)),
                pl.BlockSpec((n, w), lambda s, p, *_: (s, 2 * nb + p)),
                pl.BlockSpec((n, w), lambda s, p, *_: (s, p)),
                pl.BlockSpec((n, w), lambda s, p, *_: (s, p)),
                pl.BlockSpec((1, 2 * pairs, n), lambda s, p, *_: (s * nb + p, 0, 0)),
            ],
            out_specs=pl.BlockSpec((3, n, w), lambda s, p, *_: (0, s, p)),
            scratch_shapes=[pltpu.VMEM((w, n), BF16), pltpu.VMEM(tr, BF16), pltpu.VMEM(tr, BF16), pltpu.VMEM(acc, F32), pltpu.VMEM(acc, F32)],
        ),
        out_shape=jax.ShapeDtypeStruct((3, nseq * n, width), BF16),
        compiler_params=pltpu.CompilerParams(vmem_limit_bytes=56 << 20),
        name="attn_bwd",
    )(lo, hi, segc, segr, joined, joined, joined, ctx, dctx, lse)


def ranges(segments, qt, kb):
    first = segments[:, ::qt]
    last = segments[:, qt - 1::qt]
    lo = jnp.sum(segments[:, None, :] < first[:, :, None], axis=-1, dtype=jnp.int32) // kb
    hi = (jnp.sum(segments[:, None, :] <= last[:, :, None], axis=-1, dtype=jnp.int32) + kb - 1) // kb
    return lo, hi


def layer_pass(full, tokens_in, segments, cotangent):
    (qkv_weight, query_bias, value_bias, out_weight, out_bias, norm1_gain, norm1_bias, up_weight, up_bias,
     down_weight, down_bias, norm2_gain, norm2_bias, proj_weight) = full
    width = qkv_weight.shape[0]
    gain_one = norm1_gain.astype(F32)
    gain_two = norm2_gain.astype(F32)
    bias_row = jnp.concatenate([query_bias, jnp.zeros_like(query_bias), value_bias]).astype(F32)
    joined = (nn(tokens_in, qkv_weight) + bias_row).astype(BF16)
    lo_f, hi_f = ranges(segments, 512, 256)
    context, lse = attn_fwd(joined, segments, lo_f, hi_f, qt=512, kb=256, pairs=2)
    attn_branch = nn(context, out_weight) + out_bias.astype(F32)
    first_out, first_normed, first_inverse = norm_forward(
        tokens_in.astype(F32) + attn_branch, gain_one, norm1_bias.astype(F32)
    )
    first_low = first_out.astype(BF16)
    pre_act = nn(first_low, up_weight) + up_bias.astype(F32)
    normal_cdf = 0.5 * (1.0 + lax.erf(pre_act * SQRT_HALF))
    act_low = (pre_act * normal_cdf).astype(BF16)
    act_slope = (normal_cdf + pre_act * jnp.exp(-0.5 * pre_act * pre_act) * INV_ROOT_TAU).astype(BF16)
    ffn_branch = nn(act_low, down_weight) + down_bias.astype(F32)
    second_out, second_normed, second_inverse = norm_forward(
        first_low.astype(F32) + ffn_branch, gain_two, norm2_bias.astype(F32)
    )
    second_low = second_out.astype(BF16)
    projected = nn(second_low, proj_weight)
    inv_length = lax.rsqrt(jnp.sum(projected * projected, axis=-1, keepdims=True) + EMBED_EPS)
    embedded = projected * inv_length
    grad_proj = (
        inv_length * cotangent
        - projected * inv_length**3 * jnp.sum(cotangent * projected, axis=-1, keepdims=True)
    ).astype(BF16)
    proj_grad = tn(second_low, grad_proj)
    grad_second = nt(grad_proj, proj_weight)
    gain_two_grad = jnp.sum(grad_second * second_normed, axis=0)
    shift_two_grad = jnp.sum(grad_second, axis=0)
    grad_res_two = norm_backward(grad_second, second_normed, second_inverse, gain_two)
    grad_ffn = grad_res_two.astype(BF16)
    down_bias_grad = jnp.sum(grad_ffn.astype(F32), axis=0)
    down_grad = tn(act_low, grad_ffn)
    grad_pre = (nt(grad_ffn, down_weight) * act_slope.astype(F32)).astype(BF16)
    up_bias_grad = jnp.sum(grad_pre.astype(F32), axis=0)
    up_grad = tn(first_low, grad_pre)
    grad_first = grad_res_two + nt(grad_pre, up_weight)
    gain_one_grad = jnp.sum(grad_first * first_normed, axis=0)
    shift_one_grad = jnp.sum(grad_first, axis=0)
    grad_res_one = norm_backward(grad_first, first_normed, first_inverse, gain_one)
    grad_attn = grad_res_one.astype(BF16)
    out_bias_grad = jnp.sum(grad_attn.astype(F32), axis=0)
    out_grad = tn(context, grad_attn)
    grad_context = nt(grad_attn, out_weight).astype(BF16)
    lo_b, hi_b = ranges(segments, 256, 256)
    grad_joined = attn_bwd(joined, context, grad_context, lse, segments, lo_b, hi_b, qt=256, kb=256, pairs=2, form="B")
    query_bias_grad = jnp.sum(grad_joined[0].astype(F32), axis=0)
    value_bias_grad = jnp.sum(grad_joined[2].astype(F32), axis=0)
    qkv_grad = jnp.concatenate([tn(tokens_in, grad_joined[i]) for i in range(3)], axis=1)
    input_grad = grad_res_one
    for i in range(3):
        input_grad = input_grad + nt(grad_joined[i], qkv_weight[:, i * width:(i + 1) * width])
    grads = (qkv_grad, query_bias_grad, value_bias_grad, out_grad, out_bias_grad, gain_one_grad, shift_one_grad,
             up_grad, up_bias_grad, down_grad, down_bias_grad, gain_two_grad, shift_two_grad, proj_grad)
    return embedded, input_grad, grads


AXES = ("grp", "shard")


def local(tokens, segments, embed_grad, *pieces):
    micro, nseq, length, width = tokens.shape
    full = tuple(lax.all_gather(piece, AXES, axis=0, tiled=True) for piece in pieces)
    embedded, input_grad, grads = layer_pass(
        full,
        tokens.reshape(micro * nseq * length, width),
        segments.reshape(micro * nseq, length),
        embed_grad.reshape(micro * nseq * length, embed_grad.shape[-1]),
    )
    reduced = lax.psum_scatter(grads, AXES, scatter_dimension=0, tiled=True)
    return (embedded.reshape(embed_grad.shape), input_grad.reshape(tokens.shape)) + tuple(reduced)


def solution(mesh):
    placed = (
        P(None, ("grp", "shard"), None, None),
        P(None, ("grp", "shard"), None),
        P(None, ("grp", "shard"), None, None),
        P(("grp", "shard"), None),
        P(("grp", "shard")),
        P(("grp", "shard")),
        P(("grp", "shard"), None),
        P(("grp", "shard")),
        P(("grp", "shard")),
        P(("grp", "shard")),
        P(("grp", "shard"), None),
        P(("grp", "shard")),
        P(("grp", "shard"), None),
        P(("grp", "shard")),
        P(("grp", "shard")),
        P(("grp", "shard")),
        P(("grp", "shard"), None),
    )
    return jax.shard_map(
        local,
        mesh=mesh,
        in_specs=placed,
        out_specs=(
            P(None, ("grp", "shard"), None, None),
            P(None, ("grp", "shard"), None, None),
            P(("grp", "shard"), None),
            P(("grp", "shard")),
            P(("grp", "shard")),
            P(("grp", "shard"), None),
            P(("grp", "shard")),
            P(("grp", "shard")),
            P(("grp", "shard")),
            P(("grp", "shard"), None),
            P(("grp", "shard")),
            P(("grp", "shard"), None),
            P(("grp", "shard")),
            P(("grp", "shard")),
            P(("grp", "shard")),
            P(("grp", "shard"), None),
        ),
        check_vma=False,
    )
```

time: 1260 us -> 910 us (0.72)
  matrix products: 582 us -> 191 us
  Pallas kernels: 0 us -> 118 us
  local copies, waits for them, and re-layouts: 128 us -> 30.3 us
  waiting for transfers between devices: 288 us -> 373 us
  other arithmetic: 82.5 us -> 26.1 us
    dot_general x198 -> x19, matrix products: 582 us -> 191 us  [the longest x7 80 us: nt(): lax.dot_general(left, right, (((1,), (1,)), ((), ())), preferred_element_...]
    pallas_call x0 -> x2, Pallas kernels: none -> 118 us  [the longest x1 69.8 us: attn_bwd(): pl.pallas_call(functools.partial(bwd_kernel, qt=qt, kb=kb, pairs=pairs, f...]
    unnamed x11, waiting for transfers between devices: 4.61 us -> 51.9 us
    unnamed x171 -> x56, local copies, waits for them, and re-layouts: 68.1 us -> 28.7 us
    all_gather x4, waiting for transfers between devices: 0.04 us -> 38 us  [local(): lax.all_gather(piece, AXES, axis=0, tiled=True)]
    convert_element_type x36 -> x10, other arithmetic: 33 us -> 3.44 us  [the longest x1 1.85 us: layer_pass(): grad_proj = (inv_length * cotangent - projected * inv_length ** 3 * jnp.s...]
    reduce_sum x30 -> x5, other arithmetic: 44.3 us -> 16.3 us  [the longest x1 6.16 us: layer_pass(): out_bias_grad = jnp.sum(grad_attn.astype(F32), axis=0)]
    slice x11 -> x4, local copies, waits for them, and re-layouts: 24 us -> 0.38 us  [the longest x2 0.19 us: ranges(): last = segments[:, qt - 1::qt]]
  transfers between devices with their start and end apart: 9 -> 9, of which waited for: 3 -> 4; matrix products, arithmetic and copies ran while one was open for 60% -> 23% of each run, Pallas kernels for 0% -> 13%
where the time goes in v1:
time: 910 us; the launch traced here: 904 us
  waiting for transfers between devices  373 us (41%)
  matrix products  191 us (21%)
  blocking collectives  151 us (17%)
  Pallas kernels  118 us (13%)
  local copies, waits for them, and re-layouts  30.3 us (3%)
  other arithmetic  26.1 us (3%)
  between operations  14.4 us (2%)
    reduce_scatter x3, waiting for transfers between devices, local(): reduced = lax.psum_scatter(grads, AXES, scatter_dimension=0, tiled=True)  283 us
    unnamed x2, blocking collectives  83.6 us
    dot_general x7, matrix products, nt(): lax.dot_general(left, right, (((1,), (1,)), ((), ())), preferred_element_...  80 us
    pallas_call x1, Pallas kernels, attn_bwd(): pl.pallas_call(functools.partial(bwd_kernel, qt=qt, kb=kb, pairs=pairs, f...  69.8 us
    all_gather x1, blocking collectives, local(): lax.all_gather(piece, AXES, axis=0, tiled=True)  67.4 us
    dot_general x5, matrix products, nn(): lax.dot_general(left, right, (((1,), (0,)), ((), ())), preferred_element_...  56 us
    dot_general x7, matrix products, tn(): lax.dot_general(left, right, (((0,), (0,)), ((), ())), preferred_element_...  55.3 us
    unnamed x11, waiting for transfers between devices  51.9 us
  transfers between devices with their start and end apart: 9, of which 4 were waited for; matrix products, arithmetic and copies ran while one was open for 23% of the time, Pallas kernels for 13%

profile of v1, /device:TPU:0, one launch (start us, length us, event | category | flops | bytes accessed | tf_op | source)
XLA Modules:
  0.0 904.5 jit_solution(4978986876537547459)
XLA Ops:
  18.6 42.6 %all-reduce.20 = (bf16[768]{0:T(1024)(128)(2,1)S(1)}, bf16[768]{0:T(1024)(128)(2,1)S(1)}, bf16[768]{0:T(1024)(128)(2,1)S(1)}, bf16[768]{0:T(1024)(128)(2,1)S(1)}...) all-reduce(bf16[768]{0:T(1024)(128)(2,1)S(1)} %dynamic-update-slice, ...), channel_id=1, replica_groups=mesh['grp'=16,'shard'=2] {'grp','shard'}, use_global_device_ids=true, to_apply=%add.1 | all-reduce | flops 9216 | bytes 36864
  63.4 67.4 %all_gather.55 = bf16[768,128]{1,0:T(8,128)(2,1)S(1)} all-gather(bf16[24,128]{1,0:T(8,128)(2,1)} %param.33), channel_id=1, replica_groups=mesh['grp'=16,'shard'=2] {'grp','shard'}, dimensions={0}, use_global_device_ids=true | all-gather | bytes 202752 | tf_op jit(solution)/shard_map/all_gather | solution.py:301
  131.9 12.4 %add_convert_fusion.q_ref.k_ref.v_ref = bf16[2048,2304]{1,0:T(8,128)(2,1)} fusion(bf16[2048,768]{1,0:T(8,128)(2,1)} %bitcast.81, bf16[768,2304]{1,0:T(8,128)(2,1)} %all-gather.5.cloned.1.call-done, f32[2304]{0:T(1024)S(1)} %maximum_convert_fusion), kind=kOutput, calls=%fused_computation.10 | convolution fusion | flops 7257194496 | bytes 16131072 | tf_op jit(solution)/shard_map/dot_general | solution.py:21
  144.3 47.9 %attn_fwd.1 = (bf16[2048,768]{1,0:T(8,128)(2,1)S(1)}, f32[6,4,1024]{2,1,0:T(4,128)S(1)}) custom-call(s32[2,2]{1,0:T(2,128)S(1)} %get-tuple-element.138.lo_ref, s32[2,2]{1,0:T(2,128)S(1)} %get-tuple-element.137.hi_ref, s32[2,1024,1]{2,1,0:T(8,128)S(1)} %copy-done.1, s32[2,1,1024]{2,1,0:T(1,128)S(1)} %copy-done.2, ...), custom_call_target="tpu_custom_call" | custom-call | tf_op jit(solution)/shard_map/attn_fwd/pallas_call | solution.py:96
  192.9 6.5 fusion.27
  203.0 20.1 %multiply_convert_fusion.1 = (bf16[2048,3072]{1,0:T(8,128)(2,1)}, f32[2048,3072]{1,0:T(8,128)}) fusion(f32[3072]{0:T(1024)S(1)} %convert_element_type.104, bf16[768,3072]{1,0:T(8,128)(2,1)} %all-gather.9.cloned.1.call-done, f32[2048,768]{1,0:T(8,128)} %copy-done.6, f32[768]{0:T(1024)S(1)} %convert_element_type.101, f32[768]{0:T(1024)S(1)} %convert_element_type.100, ...), kind=kOutput, calls=%fused_computation.8 | convolution fusion | flops 9709289472 | bytes 48793600 | tf_op jit(solution)/shard_map/dot_general | solution.py:21
  223.1 37.9 %all-gather.11.cloned.1.call-done = bf16[3072,768]{1,0:T(8,128)(2,1)} async-done(((bf16[96,768]{1,0:T(8,128)(2,1)}), bf16[3072,768]{1,0:T(8,128)(2,1)}) %all-gather.11.cloned.1.call-update) | async-done | bytes 4718608 | tf_op jit(solution)/shard_map/all_gather | solution.py:301
  261.0 15.8 %fusion.28 = (f32[2048]{0:T(1024)S(1)}, f32[2048,768]{1,0:T(8,128)S(1)}) fusion(f32[768]{0:T(1024)S(1)} %convert_element_type.106, bf16[2048,3072]{1,0:T(8,128)(2,1)} %get-tuple-element.128, bf16[3072,768]{1,0:T(8,128)(2,1)} %all-gather.11.cloned.1.call-done, f32[768]{0:T(1024)S(1)} %convert_element_type.101, f32[768]{0:T(1024)S(1)} %convert_element_type.100, ...), kind=kOutput, calls=%fused_computation.97 | convolution fusion | flops 9677830144 | bytes 29918208 | tf_op jit(solution)/shard_map/dot_general | solution.py:21
  285.3 6.1 multiply_reduce_fusion
  291.5 6.0 convert_reduce_fusion.1
  297.5 26.6 %convert_reduce_fusion = (f32[3072]{0:T(1024)S(1)}, bf16[2048,3072]{1,0:T(8,128)(2,1)}) fusion(f32[2048,3072]{1,0:T(8,128)} %get-tuple-element.129, f32[3072]{0:T(1024)S(1)} %convert_element_type.104, bf16[3072,768]{1,0:T(8,128)(2,1)} %all-gather.11.cloned.1.call-done, f32[2048,768]{1,0:T(8,128)S(1)} %get-tuple-element.119), kind=kOutput, calls=%fused_computation.6 | convolution fusion | flops 9759618048 | bytes 48783360 | tf_op jit(solution)/shard_map/dot_general | solution.py:25
  324.1 20.3 %multiply_reduce_fusion.1 = (f32[768]{0:T(1024)S(1)}, f32[2048]{0:T(1024)S(1)}, f32[2048]{0:T(1024)S(1)}, f32[768]{0:T(1024)S(1)}, f32[2048,768]{1,0:T(8,128)}) fusion(f32[2048,768]{1,0:T(8,128)} %copy-done.6, f32[2048]{0:T(1024)S(1)} %add_rsqrt_fusion.2, f32[2048]{0:T(1024)S(1)} %broadcast_multiply_fusion.6, f32[768]{0:T(1024)S(1)} %convert_element_type.100, ...), kind=kOutput, calls=%fused_computation.14 | convolution fusion | flops 9679398912 | bytes 36217856 | tf_op jit(solution)/shard_map/dot_general | solution.py:25
  344.4 6.2 convert_reduce_fusion.2
  357.3 7.4 convolution_convert_fusion.do_ref
  364.8 69.8 %attn_bwd.1 = bf16[3,2048,768]{2,1,0:T(8,128)(2,1)} custom-call(s32[2,4]{1,0:T(2,128)} %get-tuple-element.140.lo_ref, s32[2,4]{1,0:T(2,128)} %get-tuple-element.139.hi_ref, s32[2,1024,1]{2,1,0:T(8,128)} %broadcast_in_dim_reshape.5.segc_ref, s32[2,1,1024]{2,1,0:T(1,128)} %segr_ref.3, bf16[2048,2304]{1,0:T(8,128)(2,1)} %add_convert_fusion.q_ref.k_ref.v_ref, ...), custom_call_target="tpu_custom_call" | custom-call | tf_op jit(solution)/shard_map/attn_bwd/pallas_call | solution.py:202
  451.7 8.0 copy.51
  459.8 17.4 %fusion.24 = f32[3072,768]{1,0:T(8,128)} fusion(bf16[2048,3072]{1,0:T(8,128)(2,1)} %get-tuple-element.128, f32[2048,768]{1,0:T(8,128)} %copy-done.8), kind=kOutput, calls=%fused_computation.93 | convolution fusion | flops 9665249280 | bytes 28311552 | tf_op jit(solution)/shard_map/dot_general | solution.py:29
  477.3 18.1 %fusion.29 = f32[768,3072]{1,0:T(8,128)} fusion(bf16[2048,3072]{1,0:T(8,128)(2,1)} %get-tuple-element.136, f32[2048,768]{1,0:T(8,128)} %copy-done.6, f32[768]{0:T(1024)S(1)} %convert_element_type.101, f32[768]{0:T(1024)S(1)} %convert_element_type.100, f32[2048]{0:T(1024)S(1)} %add_rsqrt_fusion.2, f32[2048]{0:T(1024)S(1)} %broadcast_multiply_fusion.6), kind=kOutput, calls=%fused_computation.98 | convolution fusion | flops 9671540736 | bytes 28334080 | tf_op jit(solution)/shard_map/dot_general | solution.py:29
  499.2 41.0 %all-reduce.19 = (f32[768]{0:T(1024)S(1)}, f32[768]{0:T(1024)S(1)}, f32[768]{0:T(1024)S(1)}, f32[768]{0:T(1024)S(1)}, f32[768]{0:T(1024)S(1)}, /*index=5*/f32[30...) all-reduce(f32[768]{0:T(1024)S(1)} %get-tuple-element.89, ...), channel_id=3, replica_groups=mesh['grp'=16,'shard'=2] {'grp','shard'}, use_global_device_ids=true, to_apply=%region_16.17.clone | all-reduce | flops 9216 | bytes 73728
  545.4 6.1 fusion.6
  556.8 8.3 add_add_fusion
  565.1 49.2 %reduce-scatter.16.cloned.1.call-done = f32[24,2304]{1,0:T(8,128)} async-done(((f32[768,2304]{1,0:T(8,128)}), f32[24,2304]{1,0:T(8,128)}) %reduce-scatter.16.cloned.1.call-update) | async-done | bytes 221200
  614.3 142.3 %reduce-scatter.14.cloned.1.call-done = f32[96,768]{1,0:T(8,128)} async-done(((f32[3072,768]{1,0:T(8,128)}), f32[96,768]{1,0:T(8,128)}) %reduce-scatter.14.cloned.1.call-update) | async-done | bytes 294928 | tf_op jit(solution)/shard_map/reduce_scatter | solution.py:308
  756.6 141.2 %reduce-scatter.12.cloned.1.call-done = f32[24,3072]{1,0:T(8,128)} async-done(((f32[768,3072]{1,0:T(8,128)}), f32[24,3072]{1,0:T(8,128)}) %reduce-scatter.12.cloned.1.call-update) | async-done | bytes 294928 | tf_op jit(solution)/shard_map/reduce_scatter | solution.py:308
  (119 shorter events, 65.4 us)
Async XLA Ops:
  7.2 124.7 %all-gather.5.cloned.1.call-start = ((), (), s32[]{:S(2)}) async-start(), calls=%async_computation.5 | async-start | bytes 3649536 | tf_op jit(solution)/shard_map/all_gather | solution.py:301
  7.9 185.0 %all-gather.7.cloned.1.call-start = ((), (), s32[]{:S(2)}) async-start(), calls=%async_computation.6 | async-start | bytes 1216512 | tf_op jit(solution)/shard_map/all_gather | solution.py:301
  8.7 194.3 %all-gather.9.cloned.1.call-start = ((), (), s32[]{:S(2)}) async-start(), calls=%async_computation.7 | async-start | bytes 4866048 | tf_op jit(solution)/shard_map/all_gather | solution.py:301
  9.4 251.6 %all-gather.11.cloned.1.call-start = ((), (), s32[]{:S(2)}) async-start(), calls=%async_computation.8 | async-start | bytes 4866048 | tf_op jit(solution)/shard_map/all_gather | solution.py:301
  10.0 555.1 %reduce-scatter.18.cloned.1.call-start = ((), (), s32[]{:S(2)}) async-start(), calls=%async_computation.13 | async-start | bytes 405504
  131.8 12.4 %copy-start.1 = (s32[2,1024,1]{2,1,0:T(8,128)S(1)}, s32[2,1024,1]{2,1,0:T(8,128)}, u32[]{:S(2)}) copy-start(s32[2,1024,1]{2,1,0:T(8,128)} %broadcast_in_dim_reshape.5.segc_ref) | copy-start | bytes 24580
  131.9 12.4 %copy-start.2 = (s32[2,1,1024]{2,1,0:T(1,128)S(1)}, s32[2,1,1024]{2,1,0:T(1,128)}, u32[]{:S(2)}) copy-start(s32[2,1,1024]{2,1,0:T(1,128)} %segr_ref.3) | copy-start | bytes 24580
  192.2 0.6 copy-start.3
  192.9 157.7 %copy-start = (bf16[2048,768]{1,0:T(8,128)(2,1)}, bf16[2048,768]{1,0:T(8,128)(2,1)S(1)}, u32[]{:S(2)}) copy-start(bf16[2048,768]{1,0:T(8,128)(2,1)S(1)} %get-tuple-element.18.ctx_ref) | copy-start | bytes 9437188
  199.4 2.7 copy-start.6
  276.9 2.7 copy-start.5
  277.7 2.0 copy-start.7
  282.7 0.8 copy-start.9
  291.5 273.6 %reduce-scatter.10.cloned.1.call-start = ((), (), s32[]{:S(2)}) async-start(), calls=%async_computation.9 | async-start | bytes 2433024 | tf_op jit(solution)/shard_map/reduce_scatter | solution.py:308
  297.5 26.6 %copy-start.8 = (f32[2048,768]{1,0:T(8,128)}, f32[2048,768]{1,0:T(8,128)S(1)}, u32[]{:S(2)}) copy-start(f32[2048,768]{1,0:T(8,128)S(1)} %get-tuple-element.119) | copy-start | bytes 18874372
  350.5 2.6 copy-start.4
  357.3 257.0 %reduce-scatter.16.cloned.1.call-start = ((), (), s32[]{:S(2)}) async-start(), calls=%async_computation.12 | async-start | bytes 7299072
  364.8 69.8 %copy-start.10 = (bf16[2,1,1024,768]{3,2,1,0:T(8,128)(2,1)S(1)}, bf16[2,1,1024,768]{3,2,1,0:T(8,128)(2,1)}, u32[]{:S(2)}) copy-start(bf16[2,1,1024,768]{3,2,1,0:T(8,128)(2,1)} %param.17) | copy-start | bytes 9437188
  459.7 296.9 %reduce-scatter.14.cloned.1.call-start = ((), (), s32[]{:S(2)}) async-start(), calls=%async_computation.11 | async-start | bytes 9732096 | tf_op jit(solution)/shard_map/reduce_scatter | solution.py:308
  477.2 420.5 %reduce-scatter.12.cloned.1.call-start = ((), (), s32[]{:S(2)}) async-start(), calls=%async_computation.10 | async-start | bytes 9732096 | tf_op jit(solution)/shard_map/reduce_scatter | solution.py:308
  545.4 11.3 %slice-start = ((s8[6291456]{0:T(1024)(128)(4,1)}), s8[4194304]{0:T(1024)(128)(4,1)S(1)}, s32[]{:S(2)}) async-start(s8[6291456]{0:T(1024)(128)(4,1)} %bitcast.71), calls=%async_computation.14 | async-start | bytes 8388608
  551.6 5.2 slice-start.1
Sparse Core Ops, SparseCore 0:
  10.9 63.2 all-gather.4
  77.1 52.8 all-gather.6
  133.0 62.7 all-gather.8
  198.5 62.4 all-gather.10
  291.6 93.5 reduce-scatter.17
  391.8 98.1 reduce-scatter.9
  496.2 118.0 reduce-scatter.15
  621.8 134.7 reduce-scatter.13
  763.1 134.6 reduce-scatter.11
